TPU v7x, 256 devices: a whole 4x4x8 slice. The times are simulated.
256 devices in a mesh: row: 32 (over z_lo, y, x), col: 8 (over z_hi, core).
Axes of the slice: x: 4, y: 4, z: 8 (z_hi: 4, z_lo: 2; z = z_hi * 2 + z_lo), core: 2. Of those that a mesh axis runs over, the one named last changes fastest.
Arguments:
- c_left: float32 [32, 8, 2048, 256], P('row', 'col'), may hold values from -6 to 6
- c_right: float32 [32, 8, 2048, 256], P('row', 'col'), may hold values from -6 to 6
- c_rank: int32 [32, 8], P('row', 'col'), may hold values from 32 to 256, as said below
- a_left: bfloat16 [32, 2, 2048, 256], P('row', None, 'col'), may hold values from -6 to 6
- a_right: bfloat16 [32, 2, 2048, 256], P('row', None, 'col'), may hold values from -0.125 to 0.125
- a_rank: int32 [32, 2], P('row'), may hold values from 32 to 256, as said below
- a_pattern: int32 [32, 2], P('row'), may hold values 0 or 1
- b_left: bfloat16 [2, 8, 2048, 256], P(None, 'col', 'row'), may hold values from -6 to 6
- b_right: bfloat16 [2, 8, 2048, 256], P(None, 'col', 'row'), may hold values from -0.375 to 0.375
- b_rank: int32 [2, 8], P(None, 'col'), may hold values from 32 to 256, as said below
- b_pattern: int32 [2, 8], P(None, 'col'), may hold values 0 or 1
- probe: bfloat16 [2, 2048, 256], replicated, may hold values from -6 to 6
- target: int32 [32, 8, 2], P('row', 'col'), may hold values from 16 to 240, as said below
Outputs:
- out_left: float32 [32, 8, 2048, 256], P('row', 'col')
- out_right: float32 [32, 8, 2048, 256], P('row', 'col')
Inputs may be any that keep to these rules, and one draw needn't show every extreme that they name: `c_rank`: every rank lies from 32 to 256; both ends are taken by some tile. `a_rank`: every rank lies from 32 to 256; both ends are taken by some tile. `b_rank`: every rank lies from 32 to 256; both ends are taken by some tile. With g(r) = max(8, r // 16): target[i, j, 0] <= c_rank[i, j] - g(c_rank[i, j]) and target[i, j, k] <= target[i, j, k - 1] - g(target[i, j, k - 1]); both ends are taken by some tile.
All inputs are finite; a program needn't handle non-finite values. No bound on the sum of `a_pattern` or of `b_pattern` on one device may be relied on, other than what follows from the above.
Results may differ from a plain program's by a relative error of at most 0.0009.
Values may be sent and summed in bfloat16 or wider, within the bound.
A program may use at most 128 MiB of HBM per device.

v0:
```python
import math
import jax
import jax.numpy as jnp
from jax import lax
from jax.sharding import PartitionSpec as P


def column_mask(count, width):
    return (jnp.arange(width, dtype=jnp.int32) < count).astype(jnp.float32)


def product_of(left, right):
    return jnp.dot(left, right, precision=lax.Precision.HIGHEST, preferred_element_type=jnp.float32)


def transposed_product(left, right):
    return lax.dot_general(
        left,
        right,
        (((0,), (0,)), ((), ())),
        precision=lax.Precision.HIGHEST,
        preferred_element_type=jnp.float32,
    )


def recompress(left, right, keep, extra, extra_right, right_probe, probe_step, tmask):
    tile = left.shape[0]
    probe_cols = probe_step.astype(jnp.float32) * tmask[None, :]
    core_c = transposed_product(right, probe_cols) * keep[:, None]
    core_b = right_probe * tmask[None, :]
    sample = product_of(left, core_c) + product_of(extra, core_b)
    gram = transposed_product(sample, sample) + jnp.diag(1.0 - tmask)
    factor = jnp.linalg.cholesky(gram)
    basis = lax.linalg.triangular_solve(
        factor, sample, left_side=False, lower=True, transpose_a=True
    )
    back_c = transposed_product(left, basis) * keep[:, None]
    back_b = transposed_product(extra, basis)
    new_right = (product_of(right, back_c) + product_of(extra_right, back_b)) / math.sqrt(tile)
    return (basis * math.sqrt(tile), new_right)


def on_device(
    c_left,
    c_right,
    c_rank,
    a_left,
    a_right,
    a_rank,
    a_pattern,
    b_left,
    b_right,
    b_rank,
    b_pattern,
    probe,
    target,
):
    width = c_left.shape[3]
    steps = probe.shape[0]
    left = c_left[0, 0]
    right = c_right[0, 0]
    keep = column_mask(c_rank[0, 0], width)
    for step in range(steps):
        a_l, a_r = (
            lax.all_gather(a_left[0, step], "col", axis=0, tiled=True),
            lax.all_gather(a_right[0, step], "col", axis=0, tiled=True),
        )
        b_r = lax.all_gather(b_right[step, 0], "row", axis=0, tiled=True)

        def add_middle(total, piece, start, a_rows=a_r):
            return lax.dot_general(
                a_rows, piece, (((0,), (0,)), ((), ())), preferred_element_type=jnp.float32
            )

        middle = add_middle(
            jnp.zeros((width, width), jnp.float32),
            lax.all_gather(b_left[step, 0], "row", axis=0, tiled=True),
            jnp.int32(0),
        )
        weight = (a_pattern[0, step] * b_pattern[step, 0]).astype(jnp.float32)
        middle = (
            middle
            * column_mask(a_rank[0, step], width)[:, None]
            * column_mask(b_rank[step, 0], width)[None, :]
            * weight
        )
        extra = product_of(a_l.astype(jnp.float32), middle)
        right_probe = lax.dot_general(
            b_r, probe[step], (((0,), (0,)), ((), ())), preferred_element_type=jnp.float32
        )
        tmask = column_mask(target[0, 0, step], width)
        left, right = recompress(
            left, right, keep, extra, b_r.astype(jnp.float32), right_probe, probe[step], tmask
        )
        keep = tmask
    return (left[None, None], right[None, None])


def solution(mesh):
    return jax.shard_map(
        on_device,
        mesh=mesh,
        in_specs=(
            P("row", "col", None, None),
            P("row", "col", None, None),
            P("row", "col"),
            P("row", None, "col", None),
            P("row", None, "col", None),
            P("row", None),
            P("row", None),
            P(None, "col", "row", None),
            P(None, "col", "row", None),
            P(None, "col"),
            P(None, "col"),
            P(),
            P("row", "col", None),
        ),
        out_specs=(P("row", "col", None, None), P("row", "col", None, None)),
        check_vma=False,
    )
```

profile of v0, /device:TPU:1, one launch (start us, length us, event | category | flops | bytes accessed | tf_op | source)
XLA Modules:
  0.0 865.4 jit_solution(7371660439607618762)
XLA Ops:
  7.2 1.5 fusion.94
  8.8 1.7 fusion.93
  10.6 1.4 fusion.95
  12.1 1.7 fusion.92
  16.5 1.3 fusion.100
  19.5 1.2 broadcast_subtract_fusion
  21.4 1.3 fusion.96
  22.7 1.3 fusion.99
  24.0 1.4 fusion.97
  25.4 1.3 fusion.98
  29.2 1.3 compare_convert_fusion
  30.5 1.2 compare_convert_fusion.3
  31.7 5.4 fusion.23
  37.1 3.3 convolution_bitcast_fusion.1
  40.4 104.2 %all-gather.23.cloned.1.call-done = bf16[1,1,2048,256]{3,2,1,0:T(8,128)(2,1)} async-done(((bf16[1,1,64,256]{3,2,1,0:T(8,128)(2,1)}), bf16[1,1,2048,256]{3,2,1,0:T(8,128)(2,1)}) %all-gather.23.cloned.1.call-update) | async-done | bytes 1048592 | tf_op jit(solution)/shard_map/all_gather | solution.py:68
  144.6 2.0 convolution_multiply_fusion.2
  146.6 53.8 %all-gather.17.cloned.1.call-done = bf16[1,1,2048,256]{3,2,1,0:T(8,128)(2,1)} async-done(((bf16[1,1,256,256]{3,2,1,0:T(8,128)(2,1)}), bf16[1,1,2048,256]{3,2,1,0:T(8,128)(2,1)}) %all-gather.17.cloned.1.call-update) | async-done | bytes 1048592 | tf_op jit(solution)/shard_map/all_gather | solution.py:66
  200.4 130.3 %all-gather.19.cloned.1.call-done = bf16[1,1,2048,256]{3,2,1,0:T(8,128)(2,1)} async-done(((bf16[1,1,64,256]{3,2,1,0:T(8,128)(2,1)}), bf16[1,1,2048,256]{3,2,1,0:T(8,128)(2,1)}) %all-gather.19.cloned.1.call-update) | async-done | bytes 1048592 | tf_op jit(solution)/shard_map/all_gather | solution.py:77
  330.7 2.0 fusion.37
  332.7 53.1 %all-gather.21.cloned.1.call-done = bf16[1,1,2048,256]{3,2,1,0:T(8,128)(2,1)} async-done(((bf16[1,1,256,256]{3,2,1,0:T(8,128)(2,1)}), bf16[1,1,2048,256]{3,2,1,0:T(8,128)(2,1)}) %all-gather.21.cloned.1.call-update) | async-done | bytes 1048592 | tf_op jit(solution)/shard_map/all_gather | solution.py:65
  385.8 3.2 fusion.54
  389.1 2.1 convolution_add_fusion.3
  391.2 1.3 copy-done.3
  392.5 2.1 convolution_add_fusion.5
  394.8 11.7 %cholesky.130 = f32[128,128]{1,0:T(8,128)S(1)} custom-call(f32[128,128]{1,0:T(8,128)S(1)} %cholesky.194), custom_call_target="Cholesky" | custom-call | tf_op jit(solution)/shard_map/jit(cholesky)/cholesky | solution.py:33
  407.2 9.8 %custom-call.13 = f32[1,128,128]{1,2,0:T(8,128)S(1)} custom-call(f32[1,128,128]{2,1,0:T(8,128)S(1)} %get-tuple-element.57), custom_call_target="InvertDiagBlocksLowerTriangular" | custom-call | tf_op jit(solution)/shard_map/jit(cholesky)/cholesky | solution.py:33
  417.5 11.7 %cholesky.147 = f32[128,128]{1,0:T(8,128)S(1)} custom-call(f32[128,128]{1,0:T(8,128)S(1)} %convolution_subtract_fusion.3), custom_call_target="Cholesky" | custom-call | tf_op jit(solution)/shard_map/jit(cholesky)/cholesky | solution.py:33
  431.3 4.0 while.4
  432.0 1.4 bitcast_dynamic-update-slice_fusion.4
  434.0 1.4 bitcast_dynamic-update-slice_fusion.4
  435.9 20.1 %custom-call.14 = f32[2,128,128]{1,2,0:T(8,128)S(1)} custom-call(f32[2,128,128]{2,1,0:T(8,128)S(1)} %get-tuple-element.18), custom_call_target="InvertDiagBlocksLowerTriangular" | custom-call | tf_op jit(solution)/shard_map/triangular_solve/custom-call.0 | solution.py:34
  456.0 2.4 fusion.40
  460.6 1.9 fusion.62
  462.6 1.9 fusion.51
  464.4 1.9 fusion.31
  466.4 2.1 fusion.2
  468.5 1.3 copy-done.5
  469.8 2.2 fusion.20
  472.1 4.8 fusion.17
  476.8 39.2 %all-gather.31.cloned.1.call-done = bf16[1,1,2048,256]{3,2,1,0:T(8,128)(2,1)} async-done(((bf16[1,1,64,256]{3,2,1,0:T(8,128)(2,1)}), bf16[1,1,2048,256]{3,2,1,0:T(8,128)(2,1)}) %all-gather.31.cloned.1.call-update) | async-done | bytes 1048592 | tf_op jit(solution)/shard_map/all_gather | solution.py:68
  516.1 2.0 convolution_multiply_fusion
  518.1 54.1 %all-gather.25.cloned.1.call-done = bf16[1,1,2048,256]{3,2,1,0:T(8,128)(2,1)} async-done(((bf16[1,1,256,256]{3,2,1,0:T(8,128)(2,1)}), bf16[1,1,2048,256]{3,2,1,0:T(8,128)(2,1)}) %all-gather.25.cloned.1.call-update) | async-done | bytes 1048592 | tf_op jit(solution)/shard_map/all_gather | solution.py:66
  572.2 130.3 %all-gather.27.cloned.1.call-done = bf16[1,1,2048,256]{3,2,1,0:T(8,128)(2,1)} async-done(((bf16[1,1,64,256]{3,2,1,0:T(8,128)(2,1)}), bf16[1,1,2048,256]{3,2,1,0:T(8,128)(2,1)}) %all-gather.27.cloned.1.call-update) | async-done | bytes 1048592 | tf_op jit(solution)/shard_map/all_gather | solution.py:77
  702.5 2.7 fusion.35
  705.2 52.5 %all-gather.29.cloned.1.call-done = bf16[1,1,2048,256]{3,2,1,0:T(8,128)(2,1)} async-done(((bf16[1,1,256,256]{3,2,1,0:T(8,128)(2,1)}), bf16[1,1,2048,256]{3,2,1,0:T(8,128)(2,1)}) %all-gather.29.cloned.1.call-update) | async-done | bytes 1048592 | tf_op jit(solution)/shard_map/all_gather | solution.py:65
  757.7 3.3 fusion.44
  761.1 3.6 convolution_add_fusion.1
  764.7 1.3 copy-done.1
  766.0 3.8 convolution_add_fusion.4
  772.4 11.7 %cholesky.164 = f32[128,128]{1,0:T(8,128)S(1)} custom-call(f32[128,128]{1,0:T(8,128)S(1)} %cholesky.197), custom_call_target="Cholesky" | custom-call | tf_op jit(solution)/shard_map/jit(cholesky)/cholesky | solution.py:33
  784.8 9.8 %custom-call.15 = f32[1,128,128]{1,2,0:T(8,128)S(1)} custom-call(f32[1,128,128]{2,1,0:T(8,128)S(1)} %get-tuple-element.49), custom_call_target="InvertDiagBlocksLowerTriangular" | custom-call | tf_op jit(solution)/shard_map/jit(cholesky)/cholesky | solution.py:33
  795.7 1.1 convolution_subtract_fusion.2
  796.8 12.1 %cholesky.181 = f32[128,128]{1,0:T(8,128)S(1)} custom-call(f32[128,128]{1,0:T(8,128)S(1)} %convolution_subtract_fusion.2), custom_call_target="Cholesky" | custom-call | tf_op jit(solution)/shard_map/jit(cholesky)/cholesky | solution.py:33
  812.0 4.0 while.5
  812.7 1.3 bitcast_dynamic-update-slice_fusion.5
  814.7 1.3 bitcast_dynamic-update-slice_fusion.5
  816.7 20.5 %custom-call.16 = f32[2,128,128]{1,2,0:T(8,128)S(1)} custom-call(f32[2,128,128]{2,1,0:T(8,128)} %copy-done.22), custom_call_target="InvertDiagBlocksLowerTriangular" | custom-call | tf_op jit(solution)/shard_map/triangular_solve/custom-call.0 | solution.py:34
  837.2 2.4 fusion.38
  839.6 1.8 convolution_subtract_fusion
  842.6 2.7 fusion.28
  845.2 1.9 fusion.19
  847.1 1.5 multiply_bitcast_fusion
  848.6 3.1 copy.23
  853.4 5.0 fusion.1
  (110 shorter events, 21.5 us)
Async XLA Ops:
  7.2 30.0 %copy-start = (f32[1,1,2048,256]{3,2,1,0:T(8,128)S(1)}, f32[1,1,2048,256]{3,2,1,0:T(8,128)}, u32[]{:S(2)}) copy-start(f32[1,1,2048,256]{3,2,1,0:T(8,128)} %param.16) | copy-start | bytes 6291460
  7.2 137.4 %all-gather.23.cloned.1.call-start = ((), (), s32[]{:S(2)}) async-start(), calls=%async_computation.3 | async-start | bytes 1081344 | tf_op jit(solution)/shard_map/all_gather | solution.py:68
  8.8 191.6 %all-gather.17.cloned.1.call-start = ((), (), s32[]{:S(2)}) async-start(), calls=%async_computation | async-start | bytes 1179648 | tf_op jit(solution)/shard_map/all_gather | solution.py:66
  10.5 320.1 %all-gather.19.cloned.1.call-start = ((), (), s32[]{:S(2)}) async-start(), calls=%async_computation.1 | async-start | bytes 1081344 | tf_op jit(solution)/shard_map/all_gather | solution.py:77
  12.0 373.8 %all-gather.21.cloned.1.call-start = ((), (), s32[]{:S(2)}) async-start(), calls=%async_computation.2 | async-start | bytes 1179648 | tf_op jit(solution)/shard_map/all_gather | solution.py:65
  13.8 502.3 %all-gather.31.cloned.1.call-start = ((), (), s32[]{:S(2)}) async-start(), calls=%async_computation.7 | async-start | bytes 1081344 | tf_op jit(solution)/shard_map/all_gather | solution.py:68
  14.4 557.8 %all-gather.25.cloned.1.call-start = ((), (), s32[]{:S(2)}) async-start(), calls=%async_computation.4 | async-start | bytes 1179648 | tf_op jit(solution)/shard_map/all_gather | solution.py:66
  14.9 687.5 %all-gather.27.cloned.1.call-start = ((), (), s32[]{:S(2)}) async-start(), calls=%async_computation.5 | async-start | bytes 1081344 | tf_op jit(solution)/shard_map/all_gather | solution.py:77
  15.7 742.0 %all-gather.29.cloned.1.call-start = ((), (), s32[]{:S(2)}) async-start(), calls=%async_computation.6 | async-start | bytes 1179648 | tf_op jit(solution)/shard_map/all_gather | solution.py:65
  21.4 19.0 %copy-start.23 = (f32[256]{0:T(256)}, f32[256]{0:T(256)S(1)}, u32[]{:S(2)}) copy-start(f32[256]{0:T(256)S(1)} %compare_convert_fusion.5) | copy-start | bytes 3076
  385.8 3.3 copy-start.15
  389.1 2.1 copy-start.9
  391.2 1.3 copy-start.3
  435.4 0.6 copy-start.26
  456.0 2.4 copy-start.4
  458.4 2.2 copy-start.10
  460.6 11.4 %copy-start.11 = (f32[2048,128]{0,1:T(8,128)}, f32[2048,128]{0,1:T(8,128)S(1)}, u32[]{:S(2)}) copy-start(f32[2048,128]{0,1:T(8,128)S(1)} %fusion.73) | copy-start | bytes 3145732
  460.6 1.9 copy-start.18
  462.6 1.9 copy-start.24
  464.4 1.9 copy-start.13
  466.4 3.5 copy-start.16
  468.5 1.3 copy-start.5
  757.7 3.3 copy-start.14
  761.1 3.6 copy-start.7
  761.1 4.9 copy-start.25
  764.7 1.3 copy-start.1
  769.8 42.2 %copy-start.27 = (s32[2,2]{1,0:T(2,128)S(1)}, s32[2,2]{1,0:T(2,128)}, u32[]{:S(2)}) copy-start(s32[2,2]{1,0:T(2,128)} %copy-done.26) | copy-start | bytes 52
  771.7 0.7 copy-start.20
  808.9 2.1 copy-start.19
  816.0 0.6 copy-start.22
  837.2 2.5 copy-start.2
  839.6 2.9 copy-start.12
  842.6 2.7 copy-start.8
  848.6 3.1 copy-start.17
  851.8 1.6 copy-start.6
  851.8 1.6 copy-start.21
Sparse Core Ops, SparseCore 0:
  9.8 134.7 all-gather.22
  147.0 53.3 all-gather.16
  202.2 128.4 all-gather.18
  332.4 53.3 all-gather.20
  387.4 128.5 all-gather.30
  517.8 54.3 all-gather.24
  574.0 128.4 all-gather.26
  704.3 53.3 all-gather.28
where the time goes:
time: 875 us; the launch traced here: 865 us
  waiting for transfers between devices  620 us (71%)
  other arithmetic  119 us (14%)
  matrix products  73.3 us (8%)
  local copies, waits for them, and re-layouts  31.6 us (4%)
  between operations  20.7 us (2%)
    all_gather x2, waiting for transfers between devices, on_device(): lax.all_gather(b_left[step, 0], 'row', axis=0, tiled=True)  261 us
    all_gather x2, waiting for transfers between devices, on_device(): b_r = lax.all_gather(b_right[step, 0], 'row', axis=0, tiled=True)  143 us
    all_gather x2, waiting for transfers between devices, on_device(): lax.all_gather(a_right[0, step], 'col', axis=0, tiled=True)  108 us
    all_gather x2, waiting for transfers between devices, on_device(): lax.all_gather(a_left[0, step], 'col', axis=0, tiled=True)  106 us
    another operation x14, other arithmetic, recompress(): factor = jnp.linalg.cholesky(gram)  69.7 us
    another operation x5, other arithmetic, recompress(): lax.linalg.triangular_solve(factor, sample, left_side=False, lower=True,...  41.6 us
    dot_general x10, matrix products, product_of(): jnp.dot(left, right, precision=lax.Precision.HIGHEST, preferred_element_t...  30.3 us
    dot_general x8, matrix products, transposed_product(): lax.dot_general(left, right, (((0,), (0,)), ((), ())), precision=lax.Prec...  21.8 us
  transfers between devices with their start and end apart: 8, of which 8 were waited for; matrix products, arithmetic and copies ran while one was open for 14% of the time, Pallas kernels for 0%

commit v1 on v0

--- a/solution.py
+++ b/solution.py
@@ -65,7 +65,10 @@
             lax.all_gather(a_left[0, step], "col", axis=0, tiled=True),
             lax.all_gather(a_right[0, step], "col", axis=0, tiled=True),
         )
-        b_r = lax.all_gather(b_right[step, 0], "row", axis=0, tiled=True)
+        b_r = jnp.concatenate(
+            lax.all_to_all(jnp.stack([b_right[step, 0]] * lax.axis_size("row")), "row", 0, 0),
+            axis=0,
+        )
 
         def add_middle(total, piece, start, a_rows=a_r):
             return lax.dot_general(

time: 875 us -> 563 us (0.64)
  waiting for transfers between devices: 620 us -> 299 us
  starting transfers between devices: 0.32 us -> 15.5 us
    all_gather x2 -> x0, waiting for transfers between devices: 143 us -> none  [on_device(): b_r = lax.all_gather(b_right[step, 0], 'row', axis=0, tiled=True)]
    all_gather x2, waiting for transfers between devices: 108 us -> 0.04 us  [on_device(): lax.all_gather(a_right[0, step], 'col', axis=0, tiled=True)]
    all_gather x2, waiting for transfers between devices: 261 us -> 190 us  [on_device(): lax.all_gather(b_left[step, 0], 'row', axis=0, tiled=True)]
    all_to_all x0 -> x2, starting transfers between devices: none -> 15.2 us  [on_device(): lax.all_to_all(jnp.stack([b_right[step, 0]] * lax.axis_size('row')), 'row...]
  transfers between devices with their start and end apart: 8 -> 8, of which waited for: 8 -> 5; matrix products, arithmetic and copies ran while one was open for 14% -> 21% of each run, Pallas kernels for 0% -> 0%
where the time goes in v1:
time: 563 us; the launch traced here: 557 us
  waiting for transfers between devices  299 us (53%)
  other arithmetic  119 us (21%)
  matrix products  73.7 us (13%)
  local copies, waits for them, and re-layouts  29.1 us (5%)
  between operations  20.8 us (4%)
  starting transfers between devices  15.5 us (3%)
    all_gather x2, waiting for transfers between devices, on_device(): lax.all_gather(b_left[step, 0], 'row', axis=0, tiled=True)  190 us
    all_gather x2, waiting for transfers between devices, on_device(): lax.all_gather(a_left[0, step], 'col', axis=0, tiled=True)  105 us
    another operation x14, other arithmetic, recompress(): factor = jnp.linalg.cholesky(gram)  69.7 us
    another operation x5, other arithmetic, recompress(): lax.linalg.triangular_solve(factor, sample, left_side=False, lower=True,...  41.4 us
    dot_general x10, matrix products, product_of(): jnp.dot(left, right, precision=lax.Precision.HIGHEST, preferred_element_t...  31.6 us
    dot_general x8, matrix products, transposed_product(): lax.dot_general(left, right, (((0,), (0,)), ((), ())), precision=lax.Prec...  21.1 us
    all_to_all x2, starting transfers between devices, on_device(): lax.all_to_all(jnp.stack([b_right[step, 0]] * lax.axis_size('row')), 'row...  15.2 us
  transfers between devices with their start and end apart: 8, of which 5 were waited for; matrix products, arithmetic and copies ran while one was open for 21% of the time, Pallas kernels for 0%

profile of v1, /device:TPU:1, one launch (start us, length us, event | category | flops | bytes accessed | tf_op | source)
XLA Modules:
  0.0 556.7 jit_solution(13705161608626912432)
XLA Ops:
  7.2 1.8 fusion.88
  9.1 1.4 fusion.89
  10.7 1.7 fusion.87
  14.3 1.1 stack.6
  15.4 9.2 %all-to-all-start = ((bf16[32,64,256]{2,1,0:T(8,128)(2,1)}), bf16[32,64,256]{2,1,0:T(8,128)(2,1)S(1)}, u32[]{:S(2)}, u32[]{:S(2)}) async-start(bf16[32,64,256]{2,1,0:T(8,128)(2,1)} %stack.6), calls=%async_computation | async-start | bytes 2097152 | tf_op jit(solution)/shard_map/all_to_all | solution.py:69
  32.0 1.2 broadcast_subtract_fusion
  34.4 1.3 compare_convert_fusion
  35.6 1.1 compare_convert_fusion.3
  36.8 5.4 fusion.23
  42.2 3.3 convolution_bitcast_fusion.1
  45.5 2.4 all-to-all-done
  47.9 1.2 stack.7
  49.2 6.0 %all-to-all-start.1 = ((bf16[32,64,256]{2,1,0:T(8,128)(2,1)}), bf16[32,64,256]{2,1,0:T(8,128)(2,1)}, u32[]{:S(2)}, u32[]{:S(2)}) async-start(bf16[32,64,256]{2,1,0:T(8,128)(2,1)} %stack.7), calls=%async_computation.1 | async-start | bytes 2097152 | tf_op jit(solution)/shard_map/all_to_all | solution.py:69
  55.2 1.7 convolution_multiply_fusion.2
  56.9 121.8 %all-gather.15.cloned.1.call-done = bf16[1,1,2048,256]{3,2,1,0:T(8,128)(2,1)} async-done(((bf16[1,1,64,256]{3,2,1,0:T(8,128)(2,1)}), bf16[1,1,2048,256]{3,2,1,0:T(8,128)(2,1)}) %all-gather.15.cloned.1.call-update) | async-done | bytes 1048592 | tf_op jit(solution)/shard_map/all_gather | solution.py:80
  178.8 2.0 fusion.37
  180.8 52.5 %all-gather.17.cloned.1.call-done = bf16[1,1,2048,256]{3,2,1,0:T(8,128)(2,1)} async-done(((bf16[1,1,256,256]{3,2,1,0:T(8,128)(2,1)}), bf16[1,1,2048,256]{3,2,1,0:T(8,128)(2,1)}) %all-gather.17.cloned.1.call-update) | async-done | bytes 1048592 | tf_op jit(solution)/shard_map/all_gather | solution.py:65
  233.3 3.2 fusion.49
  236.6 2.1 convolution_add_fusion.3
  238.7 1.3 copy-done.3
  240.0 1.9 convolution_add_fusion.5
  242.1 11.7 %cholesky.130 = f32[128,128]{1,0:T(8,128)S(1)} custom-call(f32[128,128]{1,0:T(8,128)S(1)} %cholesky.194), custom_call_target="Cholesky" | custom-call | tf_op jit(solution)/shard_map/jit(cholesky)/cholesky | solution.py:33
  254.5 9.9 %custom-call.13 = f32[1,128,128]{1,2,0:T(8,128)S(1)} custom-call(f32[1,128,128]{2,1,0:T(8,128)S(1)} %get-tuple-element.57), custom_call_target="InvertDiagBlocksLowerTriangular" | custom-call | tf_op jit(solution)/shard_map/jit(cholesky)/cholesky | solution.py:33
  265.0 11.7 %cholesky.147 = f32[128,128]{1,0:T(8,128)S(1)} custom-call(f32[128,128]{1,0:T(8,128)S(1)} %convolution_subtract_fusion.3), custom_call_target="Cholesky" | custom-call | tf_op jit(solution)/shard_map/jit(cholesky)/cholesky | solution.py:33
  278.9 4.2 while.4
  279.6 1.4 bitcast_dynamic-update-slice_fusion.4
  281.7 1.4 bitcast_dynamic-update-slice_fusion.4
  283.7 19.9 %custom-call.14 = f32[2,128,128]{1,2,0:T(8,128)S(1)} custom-call(f32[2,128,128]{2,1,0:T(8,128)S(1)} %get-tuple-element.18), custom_call_target="InvertDiagBlocksLowerTriangular" | custom-call | tf_op jit(solution)/shard_map/triangular_solve/custom-call.0 | solution.py:34
  303.5 2.4 fusion.40
  306.0 1.1 convolution_subtract_fusion.1
  307.1 1.1 fusion.68
  308.2 1.9 fusion.57
  310.1 1.9 fusion.95
  312.0 1.9 fusion.31
  313.9 2.1 fusion.2
  316.0 1.3 copy-done.5
  317.4 2.4 fusion.20
  319.8 4.8 fusion.17
  324.6 2.0 convolution_multiply_fusion
  326.7 67.7 %all-gather.21.cloned.1.call-done = bf16[1,1,2048,256]{3,2,1,0:T(8,128)(2,1)} async-done(((bf16[1,1,64,256]{3,2,1,0:T(8,128)(2,1)}), bf16[1,1,2048,256]{3,2,1,0:T(8,128)(2,1)}) %all-gather.21.cloned.1.call-update) | async-done | bytes 1048592 | tf_op jit(solution)/shard_map/all_gather | solution.py:80
  394.4 2.7 fusion.35
  397.1 52.4 %all-gather.23.cloned.1.call-done = bf16[1,1,2048,256]{3,2,1,0:T(8,128)(2,1)} async-done(((bf16[1,1,256,256]{3,2,1,0:T(8,128)(2,1)}), bf16[1,1,2048,256]{3,2,1,0:T(8,128)(2,1)}) %all-gather.23.cloned.1.call-update) | async-done | bytes 1048592 | tf_op jit(solution)/shard_map/all_gather | solution.py:65
  449.5 3.3 fusion.42
  452.8 3.6 convolution_add_fusion.1
  456.4 1.3 copy-done.1
  457.7 3.8 convolution_add_fusion.4
  464.1 11.7 %cholesky.164 = f32[128,128]{1,0:T(8,128)S(1)} custom-call(f32[128,128]{1,0:T(8,128)S(1)} %cholesky.197), custom_call_target="Cholesky" | custom-call | tf_op jit(solution)/shard_map/jit(cholesky)/cholesky | solution.py:33
  476.5 9.8 %custom-call.15 = f32[1,128,128]{1,2,0:T(8,128)S(1)} custom-call(f32[1,128,128]{2,1,0:T(8,128)S(1)} %get-tuple-element.49), custom_call_target="InvertDiagBlocksLowerTriangular" | custom-call | tf_op jit(solution)/shard_map/jit(cholesky)/cholesky | solution.py:33
  486.3 1.0 constant_dynamic-update-slice_fusion.1
  487.4 1.1 convolution_subtract_fusion.2
  488.5 11.7 %cholesky.181 = f32[128,128]{1,0:T(8,128)S(1)} custom-call(f32[128,128]{1,0:T(8,128)S(1)} %convolution_subtract_fusion.2), custom_call_target="Cholesky" | custom-call | tf_op jit(solution)/shard_map/jit(cholesky)/cholesky | solution.py:33
  503.3 3.8 while.5
  503.9 1.3 bitcast_dynamic-update-slice_fusion.5
  505.8 1.3 bitcast_dynamic-update-slice_fusion.5
  507.8 20.5 %custom-call.16 = f32[2,128,128]{1,2,0:T(8,128)S(1)} custom-call(f32[2,128,128]{2,1,0:T(8,128)} %copy-done.21), custom_call_target="InvertDiagBlocksLowerTriangular" | custom-call | tf_op jit(solution)/shard_map/triangular_solve/custom-call.0 | solution.py:34
  528.3 2.4 fusion.38
  530.7 1.8 convolution_subtract_fusion
  532.5 1.1 fusion.64
  533.7 2.0 fusion.28
  535.6 1.9 fusion.19
  537.5 1.5 multiply_bitcast_fusion
  539.0 3.1 copy.23
  542.1 2.4 convolution_bitcast_fusion
  544.6 5.0 fusion.1
  (118 shorter events, 18.8 us)
Async XLA Ops:
  7.2 35.0 %copy-start = (f32[1,1,2048,256]{3,2,1,0:T(8,128)S(1)}, f32[1,1,2048,256]{3,2,1,0:T(8,128)}, u32[]{:S(2)}) copy-start(f32[1,1,2048,256]{3,2,1,0:T(8,128)} %param.16) | copy-start | bytes 6291460
  7.2 49.7 %all-gather.13.cloned.1.call-start = ((), (), s32[]{:S(2)}) async-start(), calls=%async_computation.2 | async-start | bytes 1179648 | tf_op jit(solution)/shard_map/all_gather | solution.py:66
  9.1 169.7 %all-gather.15.cloned.1.call-start = ((), (), s32[]{:S(2)}) async-start(), calls=%async_computation.3 | async-start | bytes 1081344 | tf_op jit(solution)/shard_map/all_gather | solution.py:80
  10.5 14.7 %copy-start.24 = (s32[1,2]{1,0:T(1,128)S(1)}, s32[1,2]{1,0:T(1,128)}, u32[]{:S(2)}) copy-start(s32[1,2]{1,0:T(1,128)} %param.22) | copy-start | bytes 28
  10.6 15.9 %copy-start.25 = (s32[2,1]{0,1:T(1,128)S(1)}, s32[2,1]{0,1:T(1,128)}, u32[]{:S(2)}) copy-start(s32[2,1]{0,1:T(1,128)} %param.26) | copy-start | bytes 28
  10.6 19.0 %copy-start.26 = (s32[1,1,2]{2,1,0:T(1,128)S(1)}, s32[1,1,2]{2,1,0:T(1,128)}, u32[]{:S(2)}) copy-start(s32[1,1,2]{2,1,0:T(1,128)} %param.28) | copy-start | bytes 28
  10.6 22.6 %copy-start.27 = (s32[1,2]{1,0:T(1,128)S(1)}, s32[1,2]{1,0:T(1,128)}, u32[]{:S(2)}) copy-start(s32[1,2]{1,0:T(1,128)} %param.21) | copy-start | bytes 28
  10.6 23.2 %copy-start.28 = (s32[2,1]{0,1:T(1,128)S(1)}, s32[2,1]{0,1:T(1,128)}, u32[]{:S(2)}) copy-start(s32[2,1]{0,1:T(1,128)} %param.25) | copy-start | bytes 28
  10.6 222.7 %all-gather.17.cloned.1.call-start = ((), (), s32[]{:S(2)}) async-start(), calls=%async_computation.4 | async-start | bytes 1179648 | tf_op jit(solution)/shard_map/all_gather | solution.py:65
  12.4 314.3 %all-gather.19.cloned.1.call-start = ((), (), s32[]{:S(2)}) async-start(), calls=%async_computation.5 | async-start | bytes 1179648 | tf_op jit(solution)/shard_map/all_gather | solution.py:66
  12.9 381.4 %all-gather.21.cloned.1.call-start = ((), (), s32[]{:S(2)}) async-start(), calls=%async_computation.6 | async-start | bytes 1081344 | tf_op jit(solution)/shard_map/all_gather | solution.py:80
  15.4 32.5 %all-to-all-start = ((bf16[32,64,256]{2,1,0:T(8,128)(2,1)}), bf16[32,64,256]{2,1,0:T(8,128)(2,1)S(1)}, u32[]{:S(2)}, u32[]{:S(2)}) async-start(bf16[32,64,256]{2,1,0:T(8,128)(2,1)} %stack.6), calls=%async_computation | async-start | bytes 2097152 | tf_op jit(solution)/shard_map/all_to_all | solution.py:69
  24.6 424.8 %all-gather.23.cloned.1.call-start = ((), (), s32[]{:S(2)}) async-start(), calls=%async_computation.7 | async-start | bytes 1179648 | tf_op jit(solution)/shard_map/all_gather | solution.py:65
  33.2 12.3 %copy-start.22 = (f32[256]{0:T(256)}, f32[256]{0:T(256)S(1)}, u32[]{:S(2)}) copy-start(f32[256]{0:T(256)S(1)} %compare_convert_fusion.5) | copy-start | bytes 3076
  47.9 9.0 %copy-start.13 = (bf16[32,64,256]{2,1,0:T(8,128)(2,1)}, bf16[32,64,256]{2,1,0:T(8,128)(2,1)S(1)}, u32[]{:S(2)}) copy-start(bf16[32,64,256]{2,1,0:T(8,128)(2,1)S(1)} %all-to-all-done) | copy-start | bytes 3145732
  49.2 275.5 %all-to-all-start.1 = ((bf16[32,64,256]{2,1,0:T(8,128)(2,1)}), bf16[32,64,256]{2,1,0:T(8,128)(2,1)}, u32[]{:S(2)}, u32[]{:S(2)}) async-start(bf16[32,64,256]{2,1,0:T(8,128)(2,1)} %stack.7), calls=%async_computation.1 | async-start | bytes 2097152 | tf_op jit(solution)/shard_map/all_to_all | solution.py:69
  233.3 3.3 copy-start.16
  236.6 2.1 copy-start.9
  238.7 1.3 copy-start.3
  283.1 0.6 copy-start.30
  303.5 2.4 copy-start.4
  306.0 2.2 copy-start.10
  308.1 11.7 %copy-start.11 = (f32[2048,128]{0,1:T(8,128)}, f32[2048,128]{0,1:T(8,128)S(1)}, u32[]{:S(2)}) copy-start(f32[2048,128]{0,1:T(8,128)S(1)} %fusion.68) | copy-start | bytes 3145732
  308.2 1.9 copy-start.14
  310.1 1.9 copy-start.23
  312.0 1.9 copy-start.15
  313.9 3.5 copy-start.18
  316.0 1.3 copy-start.5
  449.5 3.3 copy-start.17
  452.8 3.6 copy-start.7
  452.8 4.9 copy-start.29
  456.4 1.3 copy-start.1
  461.5 41.8 %copy-start.31 = (s32[2,2]{1,0:T(2,128)S(1)}, s32[2,2]{1,0:T(2,128)}, u32[]{:S(2)}) copy-start(s32[2,2]{1,0:T(2,128)} %copy-done.30) | copy-start | bytes 52
  463.4 0.7 copy-start.20
  500.5 1.8 copy-start.19
  507.1 0.7 copy-start.21
  528.2 2.5 copy-start.2
  530.7 2.9 copy-start.12
  533.7 2.0 copy-start.8
  542.1 2.4 copy-start.6
Sparse Core Ops, SparseCore 0:
  9.8 36.1 all-gather.12
  47.9 130.8 all-gather.14
  180.6 52.6 all-gather.16
  235.0 27.9 all-gather.18
  264.7 129.6 all-gather.20
  396.1 53.3 all-gather.22
